TPU v7x, 32 devices: a whole 2x2x4 slice. The times are simulated.
32 devices in a mesh: res: 4 (over x, core), blk: 8 (over z, y).
Axes of the slice: x: 2, y: 2, z: 4, core: 2. Of those that a mesh axis runs over, the one named last changes fastest.
Arguments:
- modes: float32 [2, 8, 4194304], P(None, 'res', 'blk'), may hold values from -0.078125 to 0.078125
Outputs:
- product_modes: float32 [2, 8, 4194304], P(None, 'res', 'blk')
All inputs are finite; a program needn't handle non-finite values.
Results may differ from a plain program's by a relative error of at most 0.000098.
Values sent between devices are 32-bit elements; how exact they have to be, the bound alone decides.
No kernel may reach another device: no remote copies, remote signals or barrier semaphores. Data moves between devices by JAX's collectives and lax.ppermute only.
A program may use at most 192 MiB of HBM per device.

v0:
```python
import math

import jax
import jax.numpy as jnp
from jax import lax
from jax.sharding import PartitionSpec as P

INNER = 512
EIGHTH = 4194304
SUBLEN = 12582912
PADDED = 50331648


highest = lax.Precision.HIGHEST


def grid_index(shape, axis_number):
    return lax.broadcasted_iota(jnp.int32, shape, axis_number)


def rotation(position, period, direction, factor):
    angle = direction * 2.0 * math.pi / period * (position % period).astype(jnp.float32)
    return jnp.stack([factor * jnp.cos(angle), factor * jnp.sin(angle)])


def times(left, right):
    return jnp.stack(
        [left[0] * right[0] - left[1] * right[1], left[0] * right[1] + left[1] * right[0]]
    )


def table_pair(length):
    rows = grid_index((length, length), 0)
    columns = grid_index((length, length), 1)
    angle = 2.0 * math.pi / length * (rows * columns % length).astype(jnp.float32)
    cosine = jnp.cos(angle)
    sine = jnp.sin(angle)
    forward = jnp.stack([jnp.stack([cosine, -sine], 1), jnp.stack([sine, cosine], 1)])
    backward = jnp.stack([jnp.stack([cosine, sine], 1), jnp.stack([-sine, cosine], 1)])
    return (forward, backward)


def fold_eighths(every, residue):
    parity = residue % 2
    quarter = jnp.stack([(1 - parity) * (1 - residue), parity * (2 - residue)]).astype(jnp.float32)
    quarter = quarter.reshape((2,) + (1,) * (every.ndim - 1))
    flipped = (1 - 2 * parity).astype(jnp.float32)
    padding = jnp.zeros_like(every[:, 0:1])
    upper = jnp.concatenate([every[:, 6:8], padding], axis=1)
    return every[:, 0:3] + times(quarter, every[:, 3:6]) + flipped * upper


def on_device(modes):
    width = modes.shape[2]
    blocks = lax.axis_size("blk")
    block = lax.axis_index("blk")
    residue = lax.axis_index("res")
    narrow = width // blocks
    outer = width // INNER
    first_len = 3 * blocks
    first_pair = table_pair(first_len)
    outer_pair = table_pair(outer)
    inner_pair = table_pair(INNER)
    moved_in = lax.all_to_all(
        modes.reshape(2, 2, blocks, narrow), "blk", split_axis=2, concat_axis=2, tiled=True
    )
    every = lax.all_gather(moved_in, "res", axis=1, tiled=True)
    shape = (3, blocks, narrow)
    position = (
        EIGHTH * grid_index(shape, 0)
        + width * grid_index(shape, 1)
        + block * narrow
        + grid_index(shape, 2)
    )
    spread = times(rotation(residue * position, PADDED, 1.0, 1.0), fold_eighths(every, residue))
    gathered = spread.reshape(2, first_len, narrow)
    section = jnp.einsum("akbj,bjr->akr", first_pair[0], gathered, precision=highest)
    freq_ids = grid_index((first_len, narrow), 0)
    column_ids = block * narrow + grid_index((first_len, narrow), 1)
    section = times(rotation(freq_ids * column_ids, SUBLEN, 1.0, 1.0), section)
    back = lax.all_to_all(
        section.reshape(2, blocks, 3, narrow), "blk", split_axis=1, concat_axis=3, tiled=True
    )
    local = back.reshape(2, 3, outer, INNER)
    local = jnp.einsum("asbp,bxpc->axsc", outer_pair[0], local, precision=highest)
    inner_turn = rotation(
        grid_index((outer, INNER), 0) * grid_index((outer, INNER), 1), width, 1.0, 1.0
    )
    inner_turn = inner_turn.reshape(2, 1, outer, INNER)
    local = times(inner_turn, local)
    values = jnp.einsum("akbj,bxsj->axsk", inner_pair[0], local, precision=highest)
    squared = jnp.stack(
        [values[0] * values[0] - values[1] * values[1], 2.0 * values[0] * values[1]]
    )
    local = jnp.einsum("akbj,bxsj->axsk", inner_pair[1], squared, precision=highest)
    local = times(jnp.stack([inner_turn[0], -inner_turn[1]]), local)
    local = jnp.einsum("asbp,bxpc->axsc", outer_pair[1], local, precision=highest).reshape(
        2, 3, width
    )
    slab_ids = 3 * block + grid_index((3, width), 0)
    local = times(rotation(slab_ids * grid_index((3, width), 1), SUBLEN, -1.0, 1.0), local)
    moved = lax.all_to_all(
        local.reshape(2, 3, blocks, narrow), "blk", split_axis=2, concat_axis=1, tiled=True
    )
    inverted = jnp.einsum(
        "akbj,bjr->akr", first_pair[1], moved.reshape(2, first_len, narrow), precision=highest
    )
    home = lax.all_to_all(
        inverted.reshape(2, 3, blocks, narrow), "blk", split_axis=2, concat_axis=3, tiled=True
    )
    home = home.reshape(2, 3, width)
    picked = jnp.concatenate([home[:, 1:3], home, home], axis=1)
    place = (grid_index((8, width), 0) + 4) * EIGHTH + block * width + grid_index((8, width), 1)
    partial_value = times(rotation(residue * place, PADDED, -1.0, 1.0 / PADDED), picked)
    return lax.psum_scatter(partial_value, "res", scatter_dimension=1, tiled=True)


def solution(mesh):
    return jax.shard_map(
        on_device,
        mesh=mesh,
        in_specs=(P(None, "res", "blk"),),
        out_specs=P(None, "res", "blk"),
        check_vma=False,
    )
```

profile of v0, /device:TPU:0, one launch (start us, length us, event | category | flops | bytes accessed | tf_op | source)
XLA Modules:
  0.0 2739.0 jit_solution(15947584154978163904)
XLA Ops:
  11.0 190.2 %all_to_all.44 = f32[2,2,8,65536]{3,1,0,2:T(2,128)S(1)} all-to-all(f32[2,2,8,65536]{3,1,0,2:T(2,128)S(1)} %bitcast.138), channel_id=1, replica_groups=mesh['res'=4,'blk'=8] {'blk'}, dimensions={2} | all-to-all | bytes 16777216 | tf_op jit(solution)/shard_map/all_to_all | solution.py:64
  201.2 8.3 copy.56
  210.4 199.7 %all-gather.2.cloned.1.call-done = f32[2,8,8,65536]{3,2,1,0:T(8,128)} async-done(((f32[2,2,8,65536]{3,2,1,0:T(8,128)}), f32[2,8,8,65536]{3,2,1,0:T(8,128)}) %all-gather.2.cloned.1.call-update) | async-done | bytes 33554448 | tf_op jit(solution)/shard_map/all_gather | solution.py:67
  410.1 10.2 multiply_subtract_fusion.6
  420.3 9.2 fusion.11
  429.5 27.5 %subtract_bitcast_fusion = (f32[1,24,65536]{2,1,0:T(8,128)S(1)}, f32[1,24,65536]{2,1,0:T(8,128)S(1)}) fusion(f32[2,3,8,65536]{3,2,1,0:T(8,128)S(1)} %fusion.11, s32[]{:T(128)S(6)} %mul.723, s32[8]{0:T(128)S(1)} %iota_multiply_fusion, s32[3]{0:T(128)S(1)} %iota_multiply_fusion.1, s32[]{:T(128)S(6)} %axis_index.23), kind=kLoop, calls=%fused_computation.75 | loop fusion | flops 28311552 | bytes 25165876 | tf_op jit(solution)/shard_map/stack | solution.py:27
  457.0 11.2 convolution_bitcast_fusion.1
  468.2 28.1 %multiply_subtract_fusion.5 = (f32[1,24,65536]{2,1,0:T(8,128)}, f32[1,24,65536]{2,1,0:T(8,128)}) fusion(f32[2,24,65536]{2,1,0:T(8,128)S(1)} %convolution_bitcast_fusion.1, s32[65536]{0:T(1024)S(1)} %iota_add_fusion), kind=kLoop, calls=%fused_computation.73 | loop fusion | flops 23592960 | bytes 25427968 | tf_op jit(solution)/shard_map/sub | solution.py:28
  496.2 10.5 stack.185
  506.8 10.5 stack.186
  517.2 13.9 pad_maximum_fusion.2
  531.1 6.0 all-to-all-start.1
  545.6 9.0 fusion.83
  554.6 8.6 fusion.86
  567.1 17.7 fusion.72
  584.7 16.5 fusion.77
  601.2 22.5 fusion.26
  623.7 186.8 %all-to-all-done.1 = f32[2,8,3,65536]{3,0,2,1:T(2,128)} async-done(((f32[2,8,3,65536]{3,0,2,1:T(2,128)}), f32[2,8,3,65536]{3,0,2,1:T(2,128)}, u32[]{:S(2)}, u32[]{:S(2)}) %all-to-all-start.1) | async-done | bytes 12582944 | tf_op jit(solution)/shard_map/all_to_all | solution.py:81
  810.5 16.4 copy.57
  826.9 11.0 reshape.608
  837.9 163.0 %fusion.45 = f32[2,3,1024,512]{2,3,0,1:T(8,128)} fusion(f32[1,1024,2,1024]{3,1,2,0:T(8,128)} %get-tuple-element.28, f32[1,1024,2,1024]{3,1,2,0:T(8,128)} %get-tuple-element.23, f32[2,3,1024,512]{3,2,1,0:T(8,128)} %reshape.608), kind=kOutput, calls=%fused_computation.92 | convolution fusion | flops 77313605632 | bytes 41943040 | tf_op jit(solution)/shard_map/asbp,bxpc->axsc/dot_general | solution.py:85
  1001.0 5.7 multiply_subtract_fusion.4
  1006.7 98.2 %fusion.49 = f32[2,3,1024,512]{3,2,0,1:T(8,128)S(1)} fusion(f32[1,3,1024,512]{2,3,0,1:T(8,128)S(1)} %get-tuple-element.12, f32[1,3,1024,512]{2,3,0,1:T(8,128)S(1)} %get-tuple-element.11, f32[1,512,2,512]{3,1,2,0:T(8,128)} %get-tuple-element.30, f32[1,512,2,512]{3,1,2,0:T(8,128)} %get-tuple-element.33), kind=kOutput, calls=%fused_computation.94 | convolution fusion | flops 38658899968 | bytes 29360128 | tf_op jit(solution)/shard_map/akbj,bxsj->axsk/dot_general | solution.py:91
  1108.5 43.1 %fusion.48 = f32[2,3,1024,512]{2,3,0,1:T(8,128)S(1)} fusion(f32[1,3,1024,512]{3,2,0,1:T(8,128)} %get-tuple-element.22, f32[1,3,1024,512]{3,2,0,1:T(8,128)S(1)} %get-tuple-element.21, f32[1,512,2,512]{3,1,2,0:T(8,128)} %get-tuple-element.34, f32[1,512,2,512]{3,1,2,0:T(8,128)} %get-tuple-element.29), kind=kOutput, calls=%fused_computation.93 | convolution fusion | flops 38658899968 | bytes 29360128 | tf_op jit(solution)/shard_map/akbj,bxsj->axsk/dot_general | solution.py:95
  1151.6 5.8 multiply_subtract_fusion.2
  1157.4 88.3 %fusion.50 = f32[2,3,1024,512]{2,3,0,1:T(8,128)} fusion(f32[1,1024,2,1024]{3,1,2,0:T(8,128)} %get-tuple-element.24, f32[1,1024,2,1024]{3,1,2,0:T(8,128)} %get-tuple-element.27, f32[1,3,1024,512]{2,3,0,1:T(8,128)} %get-tuple-element.10, f32[1,3,1024,512]{2,3,0,1:T(8,128)} %get-tuple-element.9), kind=kOutput, calls=%fused_computation.95 | convolution fusion | flops 77316751360 | bytes 41943040 | tf_op jit(solution)/shard_map/asbp,bxpc->axsc/dot_general | solution.py:97
  1245.7 12.0 fusion.122
  1257.7 6.6 copy.61
  1264.4 6.9 squeeze.4
  1271.3 6.6 copy.62
  1277.9 6.8 squeeze.5
  1284.7 31.1 %multiply_subtract_fusion.1 = (f32[1,3,8,65536]{3,2,1,0:T(8,128)S(1)}, f32[1,3,8,65536]{3,2,1,0:T(8,128)}) fusion(f32[1,3,8,65536]{3,2,1,0:T(8,128)} %squeeze.5, f32[1,3,8,65536]{3,2,1,0:T(8,128)} %squeeze.4, s32[3]{0:T(128)S(1)} %copy-done.2), kind=kLoop, calls=%fused_computation.62 | loop fusion | flops 26738688 | bytes 25165836 | tf_op jit(solution)/shard_map/sub | solution.py:28
  1315.8 8.1 pad_maximum_fusion.3
  1323.9 21.9 copy.63
  1351.4 272.4 %all-to-all-done.2 = f32[2,3,8,65536]{3,0,1,2:T(2,128)} async-done(((f32[2,3,8,65536]{3,0,1,2:T(2,128)}), f32[2,3,8,65536]{3,0,1,2:T(2,128)}, u32[]{:S(2)}, u32[]{:S(2)}) %all-to-all-start.2) | async-done | bytes 12582944 | tf_op jit(solution)/shard_map/all_to_all | solution.py:102
  1623.8 22.7 convolution_bitcast_fusion
  1646.5 11.0 copy.65
  1657.5 5.4 all-to-all-start.3
  1663.1 271.5 %all-to-all-done.3 = f32[2,3,8,65536]{3,0,1,2:T(2,128)} async-done(((f32[2,3,8,65536]{3,0,1,2:T(2,128)}), f32[2,3,8,65536]{3,0,1,2:T(2,128)}, u32[]{:S(2)}, u32[]{:S(2)}) %all-to-all-start.3) | async-done | bytes 12582944 | tf_op jit(solution)/shard_map/all_to_all | solution.py:108
  1934.6 16.4 copy.90
  1950.9 21.6 reshape.628
  1972.5 10.4 slice.135
  1982.9 20.1 pad_maximum_fusion
  2003.1 76.4 %multiply_subtract_fusion = (f32[1,8,524288]{2,1,0:T(8,128)}, f32[1,8,524288]{2,1,0:T(8,128)}) fusion(f32[2,8,524288]{2,1,0:T(8,128)S(1)} %pad_maximum_fusion, s32[8]{0:T(128)S(1)} %multiply_add_fusion.7, s32[]{:T(128)S(6)} %axis_index.23), kind=kLoop, calls=%fused_computation.16 | loop fusion | flops 75497472 | bytes 67108896 | tf_op jit(solution)/shard_map/sub | solution.py:28
  2079.5 22.4 pad_maximum_fusion.1
  2101.9 54.7 %copy.70 = f32[2,8,524288]{2,0,1:T(2,128)} copy(f32[2,8,524288]{2,1,0:T(8,128)} %pad_maximum_fusion.1) | data formatting | bytes 67108864 | tf_op jit(solution)/shard_map/stack | solution.py:27
  2158.5 554.8 %all-reduce.4.cloned.1.call-done = f32[2,8,524288]{2,0,1:T(2,128)} async-done(((f32[2,8,524288]{2,0,1:T(2,128)}), f32[2,8,524288]{2,0,1:T(2,128)}) %all-reduce.4.cloned.1.call-update) | async-done | bytes 33554448
  2717.8 14.1 copy.71
  (34 shorter events, 32.7 us)
Async XLA Ops:
  6.5 403.6 %all-gather.2.cloned.1.call-start = ((), (), s32[]{:S(2)}) async-start(), calls=%async_computation.4 | async-start | bytes 41943040 | tf_op jit(solution)/shard_map/all_gather | solution.py:67
  410.1 10.2 slice-start
  531.1 279.4 %all-to-all-start.1 = ((f32[2,8,3,65536]{3,0,2,1:T(2,128)}), f32[2,8,3,65536]{3,0,2,1:T(2,128)}, u32[]{:S(2)}, u32[]{:S(2)}) async-start(f32[2,8,3,65536]{3,0,2,1:T(2,128)} %pad_maximum_fusion.2), calls=%async_computation.1 | async-start | bytes 25165824 | tf_op jit(solution)/shard_map/all_to_all | solution.py:81
  837.9 163.0 %copy-start.1 = (f32[1024,512]{0,1:T(8,128)S(1)}, f32[1024,512]{0,1:T(8,128)}, u32[]{:S(2)}) copy-start(f32[1024,512]{0,1:T(8,128)} %get-tuple-element.46) | copy-start | bytes 6291460
  1108.4 43.1 %copy-start = (f32[1024,512]{0,1:T(8,128)S(1)}, f32[1024,512]{0,1:T(8,128)}, u32[]{:S(2)}) copy-start(f32[1024,512]{0,1:T(8,128)} %fusion.86) | copy-start | bytes 6291460
  1277.9 6.8 copy-start.2
  1345.9 277.9 %all-to-all-start.2 = ((f32[2,3,8,65536]{3,0,1,2:T(2,128)}), f32[2,3,8,65536]{3,0,1,2:T(2,128)}, u32[]{:S(2)}, u32[]{:S(2)}) async-start(f32[2,3,8,65536]{3,0,1,2:T(2,128)} %copy.63), calls=%async_computation.2 | async-start | bytes 25165824 | tf_op jit(solution)/shard_map/all_to_all | solution.py:102
  1657.5 277.1 %all-to-all-start.3 = ((f32[2,3,8,65536]{3,0,1,2:T(2,128)}), f32[2,3,8,65536]{3,0,1,2:T(2,128)}, u32[]{:S(2)}, u32[]{:S(2)}) async-start(f32[2,3,8,65536]{3,0,1,2:T(2,128)} %copy.65), calls=%async_computation.3 | async-start | bytes 25165824 | tf_op jit(solution)/shard_map/all_to_all | solution.py:108
  1662.8 1050.5 %all-reduce.4.cloned.1.call-start = ((), (), s32[]{:S(2)}) async-start(), calls=%async_computation.5 | async-start | bytes 67108864
  2156.6 0.7 copy-start.3
Sparse Core Ops, SparseCore 0:
  209.6 200.4 all-gather.1
  2156.8 556.5 all-reduce.3
where the time goes:
time: 2750 us; the launch traced here: 2740 us
  waiting for transfers between devices  1490 us (54%)
  matrix products  427 us (16%)
  other arithmetic  349 us (13%)
  local copies, waits for them, and re-layouts  257 us (9%)
  blocking collectives  190 us (7%)
    unnamed x3, waiting for transfers between devices  555 us
    all_to_all x1, waiting for transfers between devices, on_device(): lax.all_to_all(local.reshape(2, 3, blocks, narrow), 'blk', split_axis=2,...  272 us
    all_to_all x1, waiting for transfers between devices, on_device(): lax.all_to_all(inverted.reshape(2, 3, blocks, narrow), 'blk', split_axis=...  271 us
    all_gather x1, waiting for transfers between devices, on_device(): every = lax.all_gather(moved_in, 'res', axis=1, tiled=True)  200 us
    all_to_all x1, blocking collectives, on_device(): lax.all_to_all(modes.reshape(2, 2, blocks, narrow), 'blk', split_axis=2,...  190 us
    all_to_all x1, waiting for transfers between devices, on_device(): lax.all_to_all(section.reshape(2, blocks, 3, narrow), 'blk', split_axis=1...  187 us
    dot_general x1, matrix products, on_device(): jnp.einsum('asbp,bxpc->axsc', outer_pair[0], local, precision=highest)  163 us
    sub x6, other arithmetic, times(): left[0] * right[0] - left[1] * right[1]  157 us
  transfers between devices with their start and end apart: 5, of which 5 were waited for; matrix products, arithmetic and copies ran while one was open for 3% of the time, Pallas kernels for 0%

commit v1 on v0

v1 whole, which is shorter than its diff:
```python
import math

import jax
import jax.numpy as jnp
from jax import lax
from jax.sharding import PartitionSpec as P

AXES = ("res", "blk")
PARTS = 12
KEPT = 8
SKIP = 4

high = lax.Precision.HIGH


def iota(shape, axis):
    return lax.broadcasted_iota(jnp.int32, shape, axis)


def unit(position, period):
    angle = 2.0 * math.pi / period * (position % period).astype(jnp.float32)
    return jnp.cos(angle), jnp.sin(angle)


def cmul(left, right):
    return (
        left[0] * right[0] - left[1] * right[1],
        left[0] * right[1] + left[1] * right[0],
    )


def real_form(pair, sign, axes=(0, 2)):
    c, s = pair
    s = sign * s
    return jnp.stack([jnp.stack([c, -s], axes[1] - 1), jnp.stack([s, c], axes[1] - 1)], axes[0])


def on_device(modes):
    width = modes.shape[2]
    blocks = lax.axis_size("blk")
    groups = lax.axis_size("res")
    devices = blocks * groups
    own = KEPT // groups
    device = lax.axis_index("res") * blocks + lax.axis_index("blk")
    first = PARTS * blocks
    mine = first // devices
    padded = first * width
    chunk = width // devices
    inner = 512
    outer = width // inner
    share = chunk // inner if chunk >= inner else 1
    low = chunk // share

    order = (own, groups, blocks)
    place = (iota(order, 1) * own + iota(order, 0)) * blocks + iota(order, 2)
    place = place.reshape(1, KEPT * blocks)
    forward = real_form(unit(iota((first, 1), 0) * place, first), 1.0)
    backward = real_form(unit(iota((first, 1), 0) * (place + SKIP * blocks), first), -1.0)

    row_u = iota((first, share), 0)
    row = unit(row_u * (device * chunk + low * iota((first, share), 1)), padded)
    col = unit(iota((first, low), 0) * iota((first, low), 1), padded)
    turn = cmul((row[0][:, :, None], row[1][:, :, None]), (col[0][:, None], col[1][:, None]))

    got = lax.all_to_all(
        modes.reshape(2, own, devices, share, low), AXES, split_axis=2, concat_axis=2, tiled=True
    )
    got = got.reshape(2, KEPT * blocks, share, low)
    section = jnp.einsum("aubm,bmxc->auxc", forward, got, precision=high)
    section = jnp.stack(cmul(turn, section))
    back = lax.all_to_all(
        section.reshape(2, devices, mine, share, low), AXES, split_axis=1, concat_axis=1, tiled=True
    )
    local = back.reshape(2, devices, mine, chunk).transpose(0, 2, 1, 3).reshape(2, mine, outer, inner)

    outer_pair = unit(iota((outer, outer), 0) * iota((outer, outer), 1), outer)
    inner_pair = unit(iota((inner, inner), 0) * iota((inner, inner), 1), inner)
    inner_turn = unit(iota((outer, inner), 0) * iota((outer, inner), 1), width)

    local = jnp.einsum("asbp,bxpc->axsc", real_form(outer_pair, 1.0), local, precision=high)
    local = jnp.stack(cmul(inner_turn, local))
    values = jnp.einsum("akbj,bxsj->axsk", real_form(inner_pair, 1.0), local, precision=high)
    squared = jnp.stack(
        [(values[0] - values[1]) * (values[0] + values[1]), 2.0 * values[0] * values[1]]
    )
    local = jnp.einsum("akbj,bxsj->axsk", real_form(inner_pair, -1.0), squared, precision=high)
    local = jnp.stack(cmul((inner_turn[0], -inner_turn[1]), local))
    local = jnp.einsum("asbp,bxpc->axsc", real_form(outer_pair, -1.0), local, precision=high)

    moved = lax.all_to_all(
        local.reshape(2, mine, devices, share, low).transpose(0, 2, 1, 3, 4),
        AXES, split_axis=1, concat_axis=1, tiled=True,
    )
    moved = moved.reshape(2, first, share, low)
    moved = jnp.stack(cmul((turn[0] * (1.0 / padded), turn[1] * (-1.0 / padded)), moved))
    result = jnp.einsum(
        "aubm,buxc->amxc", backward, moved, precision=high
    )
    home = lax.all_to_all(
        result.reshape(2, own, devices, share, low), AXES, split_axis=2, concat_axis=2, tiled=True
    )
    return home.reshape(2, own, width)


def solution(mesh):
    return jax.shard_map(
        on_device,
        mesh=mesh,
        in_specs=(P(None, "res", "blk"),),
        out_specs=P(None, "res", "blk"),
        check_vma=False,
    )
```

time: 2750 us -> 1390 us (0.51)
  waiting for transfers between devices: 1490 us -> 645 us
  other arithmetic: 349 us -> 147 us
  matrix products: 427 us -> 231 us
  local copies, waits for them, and re-layouts: 257 us -> 159 us
    unnamed x3 -> x0, waiting for transfers between devices: 555 us -> none
    all_gather x1 -> x0, waiting for transfers between devices: 200 us -> none  [on_device(): every = lax.all_gather(moved_in, 'res', axis=1, tiled=True)]
    dot_general x6, matrix products: 427 us -> 231 us  [the longest x1 86 us: on_device(): jnp.einsum('asbp,bxpc->axsc', real_form(outer_pair, 1.0), local, precisio...]
    sub x7 -> x4, other arithmetic: 161 us -> 25.9 us  [cmul(): left[0] * right[0] - left[1] * right[1]]
    all_to_all x3, waiting for transfers between devices: 731 us -> 645 us  [the longest x1 282 us: on_device(): lax.all_to_all(local.reshape(2, mine, devices, share, low).transpose(0, 2...]
    another operation x4 -> x1, local copies, waits for them, and re-layouts: 97.6 us -> 12 us  [on_device(): section = jnp.stack(cmul(turn, section))]
    another operation x7 -> x5, other arithmetic: 98.3 us -> 36.2 us  [the longest x4 26.7 us: real_form(): jnp.stack([jnp.stack([c, -s], axes[1] - 1), jnp.stack([s, c], axes[1] - 1...]
    reshape x4 -> x6, local copies, waits for them, and re-layouts: 53.5 us -> 73.9 us  [the longest x2 27.6 us: on_device(): back.reshape(2, devices, mine, chunk).transpose(0, 2, 1, 3)]
  transfers between devices with their start and end apart: 5 -> 3, of which waited for: 5 -> 3; matrix products, arithmetic and copies ran while one was open for 3% -> 8% of each run, Pallas kernels for 0% -> 0%
where the time goes in v1:
time: 1390 us
  waiting for transfers between devices  645 us (46%)
  matrix products  231 us (17%)
  blocking collectives  187 us (13%)
  local copies, waits for them, and re-layouts  159 us (11%)
  other arithmetic  147 us (11%)
  starting transfers between devices  15.7 us (1%)
    all_to_all x1, waiting for transfers between devices, on_device(): lax.all_to_all(local.reshape(2, mine, devices, share, low).transpose(0, 2...  282 us
    all_to_all x1, waiting for transfers between devices, on_device(): lax.all_to_all(modes.reshape(2, own, devices, share, low), AXES, split_ax...  188 us
    all_to_all x1, blocking collectives, on_device(): lax.all_to_all(result.reshape(2, own, devices, share, low), AXES, split_a...  187 us
    all_to_all x1, waiting for transfers between devices, on_device(): lax.all_to_all(section.reshape(2, devices, mine, share, low), AXES, split...  176 us
    dot_general x1, matrix products, on_device(): jnp.einsum('asbp,bxpc->axsc', real_form(outer_pair, 1.0), local, precisio...  86 us
    dot_general x1, matrix products, on_device(): jnp.einsum('akbj,bxsj->axsk', real_form(inner_pair, 1.0), local, precisio...  61.4 us
    dot_general x1, matrix products, on_device(): jnp.einsum('asbp,bxpc->axsc', real_form(outer_pair, -1.0), local, precisi...  46.8 us
  transfers between devices with their start and end apart: 3, of which 3 were waited for; matrix products, arithmetic and copies ran while one was open for 8% of the time, Pallas kernels for 0%

profile of v1, /device:TPU:0, one launch (start us, length us, event | category | flops | bytes accessed | tf_op | source)
XLA Modules:
  0.0 1385.1 jit_solution(13819439389830380699)
XLA Ops:
  0.0 11.4 reshape.579
  11.4 15.4 %copy.42 = f32[2,2,32,32,512]{4,1,0,3,2:T(2,128)} copy(f32[2,2,32,32,512]{4,3,2,1,0:T(8,128)} %reshape.579) | data formatting | bytes 16777216 | tf_op jit(solution)/shard_map/reshape | solution.py:66
  26.8 7.6 all-to-all-start
  34.6 0.2 fusion.99
  34.8 0.3 copy-done.12
  35.1 0.8 fusion.71
  36.1 187.6 %all-to-all-done = f32[2,2,32,32,512]{4,1,0,3,2:T(2,128)} async-done(((f32[2,2,32,32,512]{4,1,0,3,2:T(2,128)}), f32[2,2,32,32,512]{4,1,0,3,2:T(2,128)}, u32[]{:S(2)}, u32[]{:S(2)}) %all-to-all-start) | async-done | bytes 8388640 | tf_op jit(solution)/shard_map/all_to_all | solution.py:65
  223.7 8.2 copy.43
  231.9 6.0 convolution_bitcast_fusion
  238.0 4.7 multiply_subtract_fusion.3
  242.7 6.4 copy.45
  249.1 6.3 copy.44
  255.4 9.5 pad_maximum_fusion
  265.0 12.0 copy.46
  277.0 4.2 all-to-all-start.1
  281.2 3.8 fusion.66
  285.0 4.1 fusion.64
  289.1 4.0 broadcast_multiply_fusion.1
  293.2 9.0 fusion.59
  302.2 8.6 fusion.62
  310.8 4.0 fusion.43
  314.8 16.5 %broadcast_multiply_fusion = (f32[1024,1,1024]{2,0,1:T(8,128)}, f32[1024,1,1024]{2,0,1:T(8,128)}) fusion(), kind=kLoop, calls=%fused_computation.81 | loop fusion | flops 15728640 | bytes 8388608 | tf_op jit(solution)/shard_map/mul | solution.py:34
  331.3 17.7 %fusion.48 = (f32[1024,1,1024]{2,0,1:T(8,128)}, f32[1024,1,1024]{2,0,1:T(8,128)}) fusion(), kind=kLoop, calls=%fused_computation.83 | loop fusion | flops 15728640 | bytes 8388608 | tf_op jit(solution)/shard_map/cos | solution.py:22
  348.9 16.3 %fusion.53 = f32[1024,1,1024]{2,0,1:T(8,128)} fusion(), kind=kLoop, calls=%fused_computation.88 | loop fusion | flops 16777216 | bytes 4194304 | tf_op jit(solution)/shard_map/neg | solution.py:35
  365.3 22.1 %fusion.20 = (f32[1,1024,2,1024]{3,1,2,0:T(8,128)}, f32[1,1024,2,1024]{3,1,2,0:T(8,128)}, f32[1,1024,2,1024]{3,1,2,0:T(8,128)}, f32[1,1024,2,1024]{3,1,2,0:T(8,128)}) fusion(f32[1024,1,1024]{2,0,1:T(8,128)} %get-tuple-element.39, f32[1024,1,1024]{2,0,1:T(8,128)} %get-tuple-element.40, f32[1024,1,1024]{2,0,1:T(8,128)} %get-tuple-element.37, ...), kind=kLoop, calls=%fused_computation.31 | loop fusion | flops 8388608 | bytes 54525952 | tf_op jit(solution)/shard_map/stack | solution.py:35
  387.3 175.9 %all-to-all-done.1 = f32[2,32,3,32,512]{4,3,2,0,1:T(8,128)} async-done(((f32[2,32,3,32,512]{4,3,2,0,1:T(8,128)}), f32[2,32,3,32,512]{4,3,2,0,1:T(8,128)}, u32[]{:S(2)}, u32[]{:S(2)}) %all-to-all-start.1) | async-done | bytes 12582944 | tf_op jit(solution)/shard_map/all_to_all | solution.py:71
  563.3 12.0 copy.47
  575.3 13.8 reshape.581
  589.1 13.8 reshape.582
  602.9 86.0 %fusion.24 = f32[2,3,1024,512]{2,3,0,1:T(8,128)} fusion(f32[1,1024,2,1024]{3,1,2,0:T(8,128)} %get-tuple-element.20, f32[1,1024,2,1024]{3,1,2,0:T(8,128)} %get-tuple-element.17, f32[2,3,1024,512]{3,2,1,0:T(8,128)} %reshape.582), kind=kOutput, calls=%fused_computation.50 | convolution fusion | flops 38658899968 | bytes 41943040 | tf_op jit(solution)/shard_map/asbp,bxpc->axsc/dot_general | solution.py:80
  688.9 5.7 multiply_subtract_fusion.2
  694.6 61.4 %fusion.28 = f32[2,3,1024,512]{3,2,0,1:T(8,128)S(1)} fusion(f32[1,3,1024,512]{2,3,0,1:T(8,128)S(1)} %get-tuple-element.8, f32[1,3,1024,512]{2,3,0,1:T(8,128)S(1)} %get-tuple-element.7, f32[1,512,2,512]{3,1,2,0:T(8,128)} %get-tuple-element.23, f32[1,512,2,512]{3,1,2,0:T(8,128)} %get-tuple-element.24), kind=kOutput, calls=%fused_computation.52 | convolution fusion | flops 19331547136 | bytes 29360128 | tf_op jit(solution)/shard_map/akbj,bxsj->axsk/dot_general | solution.py:82
  756.1 3.5 add_multiply_fusion
  759.6 24.9 %fusion.27 = f32[2,3,1024,512]{2,3,0,1:T(8,128)S(1)} fusion(f32[1,3,1024,512]{3,2,0,1:T(8,128)} %get-tuple-element.16, f32[1,3,1024,512]{3,2,0,1:T(8,128)S(1)} %get-tuple-element.15, f32[1,512,2,512]{3,1,2,0:T(8,128)} %get-tuple-element.22, f32[1,512,2,512]{3,1,2,0:T(8,128)} %get-tuple-element.21), kind=kOutput, calls=%fused_computation.51 | convolution fusion | flops 19331547136 | bytes 29360128 | tf_op jit(solution)/shard_map/akbj,bxsj->axsk/dot_general | solution.py:86
  784.5 5.9 multiply_subtract_fusion.1
  790.4 46.8 %fusion.29 = f32[2,3,1024,512]{2,3,0,1:T(8,128)} fusion(f32[1,1024,2,1024]{3,1,2,0:T(8,128)} %get-tuple-element.18, f32[1,1024,2,1024]{3,1,2,0:T(8,128)} %get-tuple-element.19, f32[1,3,1024,512]{2,3,0,1:T(8,128)} %get-tuple-element.6, f32[1,3,1024,512]{2,3,0,1:T(8,128)} %get-tuple-element.5), kind=kOutput, calls=%fused_computation.53 | convolution fusion | flops 38662045696 | bytes 41943040 | tf_op jit(solution)/shard_map/asbp,bxpc->axsc/dot_general | solution.py:88
  837.2 13.0 copy.51
  850.3 12.0 copy.52
  862.3 3.9 all-to-all-start.2
  866.5 0.7 maximum_bitcast_fusion.28
  867.2 281.6 %all-to-all-done.2 = f32[2,32,3,32,512]{4,3,2,0,1:T(8,128)} async-done(((f32[2,32,3,32,512]{4,3,2,0,1:T(8,128)}), f32[2,32,3,32,512]{4,3,2,0,1:T(8,128)}, u32[]{:S(2)}, u32[]{:S(2)}) %all-to-all-start.2) | async-done | bytes 12582944 | tf_op jit(solution)/shard_map/all_to_all | solution.py:90
  1148.7 9.5 fusion.106
  1158.3 9.6 multiply_subtract_fusion
  1167.9 5.7 fusion.14
  1173.6 8.1 copy.60
  1181.7 186.8 %all_to_all.20 = f32[2,2,32,32,512]{4,1,3,0,2:T(2,128)S(1)} all-to-all(f32[2,2,32,32,512]{4,1,3,0,2:T(2,128)S(1)} %copy.60), channel_id=1, replica_groups=mesh['res'=4,'blk'=8] {'res','blk'}, dimensions={2} | all-to-all | bytes 16777216 | tf_op jit(solution)/shard_map/all_to_all | solution.py:99
  1368.5 4.9 copy.61
  1373.4 11.4 reshape.585
  (35 shorter events, 0.6 us)
Async XLA Ops:
  26.8 196.9 %all-to-all-start = ((f32[2,2,32,32,512]{4,1,0,3,2:T(2,128)}), f32[2,2,32,32,512]{4,1,0,3,2:T(2,128)}, u32[]{:S(2)}, u32[]{:S(2)}) async-start(f32[2,2,32,32,512]{4,1,0,3,2:T(2,128)} %copy.42), calls=%async_computation | async-start | bytes 16777216 | tf_op jit(solution)/shard_map/all_to_all | solution.py:65
  34.6 0.5 copy-start.12
  35.9 202.0 %copy-start.2 = (f32[96,512]{1,0:T(8,128)}, f32[96,512]{1,0:T(8,128)S(1)}, u32[]{:S(2)}) copy-start(f32[96,512]{1,0:T(8,128)S(1)} %get-tuple-element.41) | copy-start | bytes 589828
  35.9 202.0 %copy-start.4 = (f32[96,512]{1,0:T(8,128)}, f32[96,512]{1,0:T(8,128)S(1)}, u32[]{:S(2)}) copy-start(f32[96,512]{1,0:T(8,128)S(1)} %get-tuple-element.42) | copy-start | bytes 589828
  36.1 201.9 %copy-start.8 = (f32[96,32]{0,1:T(8,128)}, f32[96,32]{0,1:T(8,128)S(1)}, u32[]{:S(2)}) copy-start(f32[96,32]{0,1:T(8,128)S(1)} %get-tuple-element.32) | copy-start | bytes 36868
  36.1 201.9 %copy-start.10 = (f32[96,32]{0,1:T(8,128)}, f32[96,32]{0,1:T(8,128)S(1)}, u32[]{:S(2)}) copy-start(f32[96,32]{0,1:T(8,128)S(1)} %get-tuple-element.33) | copy-start | bytes 36868
  277.0 286.3 %all-to-all-start.1 = ((f32[2,32,3,32,512]{4,3,2,0,1:T(8,128)}), f32[2,32,3,32,512]{4,3,2,0,1:T(8,128)}, u32[]{:S(2)}, u32[]{:S(2)}) async-start(f32[2,32,3,32,512]{4,3,2,0,1:T(8,128)} %copy.46), calls=%async_computation.1 | async-start | bytes 25165824 | tf_op jit(solution)/shard_map/all_to_all | solution.py:71
  602.9 86.0 %copy-start.1 = (f32[1024,512]{0,1:T(8,128)S(1)}, f32[1024,512]{0,1:T(8,128)}, u32[]{:S(2)}) copy-start(f32[1024,512]{0,1:T(8,128)} %get-tuple-element.43) | copy-start | bytes 6291460
  759.6 24.9 %copy-start = (f32[1024,512]{0,1:T(8,128)S(1)}, f32[1024,512]{0,1:T(8,128)}, u32[]{:S(2)}) copy-start(f32[1024,512]{0,1:T(8,128)} %fusion.62) | copy-start | bytes 6291460
  862.3 3.9 copy-start.13
  862.3 286.4 %all-to-all-start.2 = ((f32[2,32,3,32,512]{4,3,2,0,1:T(8,128)}), f32[2,32,3,32,512]{4,3,2,0,1:T(8,128)}, u32[]{:S(2)}, u32[]{:S(2)}) async-start(f32[2,32,3,32,512]{4,3,2,0,1:T(8,128)} %copy.52), calls=%async_computation.2 | async-start | bytes 25165824 | tf_op jit(solution)/shard_map/all_to_all | solution.py:90
  867.2 291.1 %copy-start.3 = (f32[96,512]{1,0:T(8,128)S(1)}, f32[96,512]{1,0:T(8,128)}, u32[]{:S(2)}) copy-start(f32[96,512]{1,0:T(8,128)} %copy-done.2) | copy-start | bytes 589828
  867.2 291.1 %copy-start.5 = (f32[96,512]{1,0:T(8,128)S(1)}, f32[96,512]{1,0:T(8,128)}, u32[]{:S(2)}) copy-start(f32[96,512]{1,0:T(8,128)} %copy-done.4) | copy-start | bytes 589828
  867.2 291.1 %copy-start.9 = (f32[96,32]{0,1:T(8,128)S(1)}, f32[96,32]{0,1:T(8,128)}, u32[]{:S(2)}) copy-start(f32[96,32]{0,1:T(8,128)} %copy-done.8) | copy-start | bytes 36868
  867.2 291.1 %copy-start.11 = (f32[96,32]{0,1:T(8,128)S(1)}, f32[96,32]{0,1:T(8,128)}, u32[]{:S(2)}) copy-start(f32[96,32]{0,1:T(8,128)} %copy-done.10) | copy-start | bytes 36868
  1158.3 9.6 copy-start.6
  1158.3 9.6 copy-start.7
